TPU v7x, 128 devices: a whole 4x4x4 slice. The times are simulated.
128 devices in a mesh: grp: 8 (over x, core), dev: 16 (over y, z).
Axes of the slice: x: 4, y: 4, z: 4, core: 2. Of those that a mesh axis runs over, the one named last changes fastest.
Arguments:
- parent_state: float32 [24, 512, 2048], P(None, 'grp', 'dev'), may hold values from -6 to 6
- nest_state: float32 [16, 24, 384, 384], P('grp', None, 'dev'), may hold values from -6 to 6
- nest_anchor: int32 [16, 2], replicated, may hold values from 0 to 1920, as said below
- diffusion: float32 [2, 24], replicated, may hold values from 0.02 to 0.05
- courant: float32 [2, 24], replicated, may hold values from 0.05 to 0.15
Outputs:
- parent_out: float32 [24, 512, 2048], P(None, 'grp', 'dev')
- nest_out: float32 [16, 24, 384, 384], P('grp', None, 'dev')
Inputs may be any that keep to these rules, and one draw needn't show every extreme that they name: `nest_anchor`: the parent grid is cut into 2 x 16 / 2 disjoint bands of 256 x 256 cells; each nest lies in a band of its own, its 128 x 128 covered cells inside that band.
All inputs are finite; a program needn't handle non-finite values.
Results may differ from a plain program's by a relative error of at most 0.0003.
Values sent between devices are 32-bit elements; how exact they have to be, the bound alone decides.
A program may use at most 320 MiB of HBM per device.

v0:
```python
import jax
import jax.numpy as jnp
from jax import lax
from jax.sharding import PartitionSpec as P


def padded_2(shard, sides, width):
    for axis, dim in sides:
        size, length = (lax.axis_size(axis), shard.shape[dim])
        up = [(i, (i + 1) % size) for i in range(size - 1)]
        down = [(j, i) for i, j in up]
        last = lax.slice_in_dim(shard, length - width, length, axis=dim)
        initial = lax.slice_in_dim(shard, 0, width, axis=dim)
        before = lax.ppermute(last, axis, up)
        after = lax.ppermute(initial, axis, down)
        shard = jnp.concatenate([before, shard, after], axis=dim)
    return shard


def stencil(padded, diff_x, diff_y, adv_x, adv_y):
    centre = padded[..., 1:-1, 1:-1]
    eastern = padded[..., 1:-1, 2:]
    western = padded[..., 1:-1, :-2]
    northern = padded[..., 2:, 1:-1]
    southern = padded[..., :-2, 1:-1]
    return (
        centre
        + diff_x * (eastern - 2.0 * centre + western)
        + diff_y * (northern - 2.0 * centre + southern)
        - adv_x * (centre - western)
        - adv_y * (centre - southern)
    )


def impose(extended, row_index, south_fine, north_fine, total_rows):
    below = (row_index < 0)[None, None, :, None]
    above = (row_index >= total_rows)[None, None, :, None]
    extended = jnp.where(below, south_fine[:, :, None, :], extended)
    return jnp.where(above, north_fine[:, :, None, :], extended)


def substep_once(
    extended, row_index, west_full, east_full, south_fine, north_fine, total_rows, coefficients
):
    row_count = extended.shape[2]
    first_row = row_index[0] + 3
    west_col = lax.dynamic_slice_in_dim(west_full, first_row, row_count, 2)
    east_col = lax.dynamic_slice_in_dim(east_full, first_row, row_count, 2)
    padded = jnp.concatenate([west_col[..., None], extended, east_col[..., None]], axis=3)
    advanced = stencil(padded, coefficients[0], coefficients[1], coefficients[2], coefficients[3])
    inner_rows = row_index[1:-1]
    return (impose(advanced, inner_rows, south_fine, north_fine, total_rows), inner_rows)


def shards(parent_state, nest_state, nest_anchor, diffusion, courant):
    channels, tile_rows, tile_cols = parent_state.shape
    local_nests = nest_state.shape[0]
    nest_rows_dev = nest_state.shape[2]
    fine_cols = nest_state.shape[3]
    dev_count = lax.axis_size("dev")
    grp_index = lax.axis_index("grp")
    dev_index = lax.axis_index("dev")
    total_rows = nest_rows_dev * dev_count
    foot_rows = total_rows // 3
    foot_cols = fine_cols // 3
    nest_count = nest_anchor.shape[0]
    diff_x = diffusion[0][:, None, None]
    diff_y = diffusion[1][:, None, None]
    adv_x = courant[0][:, None, None]
    adv_y = courant[1][:, None, None]
    nest_coefficients = (3.0 * diff_x, 3.0 * diff_y, adv_x, adv_y)
    row_base = grp_index * tile_rows
    col_base = dev_index * tile_cols
    highest = lax.Precision.HIGHEST
    row_anchor = nest_anchor[:, 0:1]
    col_anchor = nest_anchor[:, 1:2]
    along_rows = jnp.arange(foot_rows, dtype=jnp.int32)[None, :]
    along_cols = jnp.arange(foot_cols, dtype=jnp.int32)[None, :]
    rows_here = row_base + jnp.arange(tile_rows, dtype=jnp.int32)
    cols_here = col_base + jnp.arange(tile_cols, dtype=jnp.int32)
    side_cols = jnp.concatenate([col_anchor - 1, col_anchor + foot_cols], axis=0)
    column_pick = (side_cols == cols_here[None, :]).astype(jnp.float32)
    column_values = jnp.einsum("cyx,mx->cym", parent_state, column_pick, precision=highest)
    row_span = ((row_anchor + along_rows)[:, :, None] == rows_here[None, None, :]).astype(
        jnp.float32
    )
    west_part = jnp.einsum(
        "nky,cyn->cnk", row_span, column_values[:, :, :nest_count], precision=highest
    )
    east_part = jnp.einsum(
        "nky,cyn->cnk", row_span, column_values[:, :, nest_count:], precision=highest
    )
    side_rows = jnp.concatenate([row_anchor - 1, row_anchor + foot_rows], axis=0)
    row_pick = (side_rows == rows_here[None, :]).astype(jnp.float32)
    row_values = jnp.einsum("my,cyx->cmx", row_pick, parent_state, precision=highest)
    col_span = ((col_anchor + along_cols)[:, :, None] == cols_here[None, None, :]).astype(
        jnp.float32
    )
    south_part = jnp.einsum("nkx,cnx->cnk", col_span, row_values[:, :nest_count], precision=highest)
    north_part = jnp.einsum("nkx,cnx->cnk", col_span, row_values[:, nest_count:], precision=highest)
    contrib = jnp.concatenate([west_part, east_part, south_part, north_part], axis=2)
    cycle_every = lax.psum(contrib, ("grp", "dev"))
    cycle_local = lax.dynamic_slice_in_dim(cycle_every, grp_index * local_nests, local_nests, 1)
    cycle_local = jnp.swapaxes(cycle_local, 0, 1)
    west_fine = jnp.repeat(cycle_local[:, :, :foot_rows], 3, axis=2)
    east_fine = jnp.repeat(cycle_local[:, :, foot_rows : 2 * foot_rows], 3, axis=2)
    west_full = jnp.pad(west_fine, ((0, 0), (0, 0), (3, 3)), mode="edge")
    east_full = jnp.pad(east_fine, ((0, 0), (0, 0), (3, 3)), mode="edge")
    south_fine = jnp.repeat(cycle_local[:, :, 2 * foot_rows : 2 * foot_rows + foot_cols], 3, axis=2)
    north_fine = jnp.repeat(cycle_local[:, :, 2 * foot_rows + foot_cols :], 3, axis=2)
    parent_pad = padded_2(parent_state, (("grp", 1), ("dev", 2)), 1)
    advanced = stencil(parent_pad, diff_x, diff_y, adv_x, adv_y)
    current = nest_state
    for substep in range(3):
        extended = padded_2(current, (("dev", 2),), 1)
        row_index = dev_index * nest_rows_dev - 1 + jnp.arange(nest_rows_dev + 2, dtype=jnp.int32)
        extended = impose(extended, row_index, south_fine, north_fine, total_rows)
        current = substep_once(
            extended,
            row_index,
            west_full,
            east_full,
            south_fine,
            north_fine,
            total_rows,
            nest_coefficients,
        )[0]
    coarse_rows = nest_rows_dev // 3
    averages = current.reshape(local_nests, channels, coarse_rows, 3, foot_cols, 3).mean(
        axis=(3, 5)
    )
    per_group = local_nests * dev_count
    zero_start = jnp.zeros((), jnp.int32)
    canvas = jnp.pad(advanced, ((0, 0), (coarse_rows, coarse_rows), (foot_cols, foot_cols)))
    pieces = lax.all_gather(averages, ("grp", "dev"), axis=0, tiled=True)
    item_count = pieces.shape[0]

    def put_one(item, canvas_inner):
        group_index = item // per_group
        member = item // local_nests % dev_count
        nest_index = group_index * local_nests + item % local_nests
        anchor = lax.dynamic_slice(nest_anchor, (nest_index, zero_start), (1, 2))
        top_at = jnp.clip(
            anchor[0, 0] + member * coarse_rows - row_base + coarse_rows, 0, tile_rows + coarse_rows
        )
        left_at = jnp.clip(anchor[0, 1] - col_base + foot_cols, 0, tile_cols + foot_cols)
        piece = lax.dynamic_index_in_dim(pieces, item, 0, keepdims=False)
        return lax.dynamic_update_slice(canvas_inner, piece, (zero_start, top_at, left_at))

    filled = lax.fori_loop(0, item_count, put_one, canvas)
    parent_out = filled[:, coarse_rows : coarse_rows + tile_rows, foot_cols : foot_cols + tile_cols]
    return (parent_out, current)


def solution(mesh):
    placed = (P(None, "grp", "dev"), P("grp", None, "dev", None), P(), P(), P())
    return jax.shard_map(
        shards,
        mesh=mesh,
        in_specs=placed,
        out_specs=(P(None, "grp", "dev"), P("grp", None, "dev", None)),
        check_vma=False,
    )
```

profile of v0, /device:TPU:95, one launch (start us, length us, event | category | flops | bytes accessed | tf_op | source)
XLA Modules:
  0.0 2034.9 jit_solution(8243158186074569799)
XLA Ops:
  22.1 138.1 %all-reduce.3.cloned.1.call-done = f32[24,16,512]{2,0,1:T(8,128)} async-done(((f32[24,16,512]{2,0,1:T(8,128)}), f32[24,16,512]{2,0,1:T(8,128)}) %all-reduce.3.cloned.1.call-update) | async-done | bytes 786448 | tf_op jit(solution)/shard_map/psum | solution.py:102
  188.6 8.9 copy.162
  197.5 10.2 reduce_sum.9
  238.1 72.8 %all-gather.2.cloned.1.call-done = f32[256,24,8,128]{3,2,1,0:T(8,128)} async-done(((f32[2,24,8,128]{3,2,1,0:T(8,128)}), f32[256,24,8,128]{3,2,1,0:T(8,128)}) %all-gather.2.cloned.1.call-update) | async-done | bytes 25165840 | tf_op jit(solution)/shard_map/all_gather | solution.py:135
  310.9 1715.1 %while.16 = (s32[]{:T(128)}, f32[24,80,384]{2,1,0:T(8,128)}, f32[256,24,8,128]{3,2,1,0:T(8,128)}, s32[16,2]{0,1:T(2,128)S(1)}, s32[]{:T(128)}, /*index=5*/s32[]{...) while((s32[]{:T(128)}, f32[24,80,384]{2,1,0:T(8,128)}, ...), condition=%wide.region_3.4_spmd, body=%wide.region_2.3_spmd.sunk | while | flops 46 | bytes 393896 | solution.py:150
  505.9 8.7 dynamic_update_slice.12
  523.4 8.7 dynamic_update_slice.12
  541.0 8.7 dynamic_update_slice.12
  558.6 8.7 dynamic_update_slice.12
  576.1 8.7 dynamic_update_slice.12
  593.7 8.7 dynamic_update_slice.12
  611.2 8.7 dynamic_update_slice.12
  628.8 8.7 dynamic_update_slice.12
  646.3 8.7 dynamic_update_slice.12
  663.9 8.7 dynamic_update_slice.12
  681.4 8.7 dynamic_update_slice.12
  699.0 8.7 dynamic_update_slice.12
  716.6 8.7 dynamic_update_slice.12
  984.8 8.7 dynamic_update_slice.12
  1002.4 8.7 dynamic_update_slice.12
  1020.0 8.7 dynamic_update_slice.12
  1037.5 8.7 dynamic_update_slice.12
  1055.1 8.7 dynamic_update_slice.12
  1072.6 8.7 dynamic_update_slice.12
  1090.2 8.7 dynamic_update_slice.12
  1107.7 8.7 dynamic_update_slice.12
  1125.3 8.7 dynamic_update_slice.12
  1142.8 8.7 dynamic_update_slice.12
  1160.4 8.7 dynamic_update_slice.12
  1178.0 8.7 dynamic_update_slice.12
  1213.1 8.7 dynamic_update_slice.12
  1230.7 8.7 dynamic_update_slice.12
  (1104 shorter events, 1223.7 us)
Async XLA Ops:
  7.2 4.3 copy-start
  7.2 153.0 %all-reduce.3.cloned.1.call-start = ((), (), s32[]{:S(2)}) async-start(), calls=%async_computation | async-start | bytes 1572864 | tf_op jit(solution)/shard_map/psum | solution.py:102
  11.9 3.1 copy-start.4
  14.9 7.1 copy-start.7
  14.9 7.2 copy-start.6
  14.9 295.9 %all-gather.2.cloned.1.call-start = ((), (), s32[]{:S(2)}) async-start(), calls=%async_computation.1 | async-start | bytes 25362432 | tf_op jit(solution)/shard_map/all_gather | solution.py:135
  15.3 1.2 copy-start.3
  16.5 147.4 %collective-permute-start.4 = (f32[2,24,1,384]{3,1,2,0:T(8,128)S(1)}, f32[2,24,1,384]{3,1,2,0:T(8,128)S(1)}, u32[]{:S(2)}, u32[]{:S(2)}) collective-permute-start(f32[2,24,1,384]{3,1,2,0:T(8,128)S(1)} %get-tuple-element.229), channel_id=1, source_target_pairs={{0,1},{1,2},{2,3},{3,4},{4,5},{5,6},{6,7},{7,8},{8,9},{9,10},{10,1... | collective-permute-start | bytes 221192 | tf_op jit(solution)/shard_map/ppermute | solution.py:14
  19.8 144.1 %collective-permute-start.5 = (f32[2,24,1,384]{3,1,2,0:T(8,128)S(1)}, f32[2,24,1,384]{3,1,2,0:T(8,128)S(1)}, u32[]{:S(2)}, u32[]{:S(2)}) collective-permute-start(f32[2,24,1,384]{3,1,2,0:T(8,128)S(1)} %get-tuple-element.230), channel_id=1, source_target_pairs={{1,0},{2,1},{3,2},{4,3},{5,4},{6,5},{7,6},{8,7},{9,8},{10,9},{11,1... | collective-permute-start | bytes 221192 | tf_op jit(solution)/shard_map/ppermute | solution.py:15
  163.9 12.5 copy-start.1
  168.2 5.8 collective-permute-start.6
  171.0 5.1 collective-permute-start.7
  178.6 5.6 collective-permute-start.8
  180.5 5.9 copy-start.2
  180.6 5.5 collective-permute-start.9
  210.0 6.6 collective-permute-start
  211.3 6.1 collective-permute-start.1
  220.5 10.5 collective-permute-start.2
  224.2 6.4 collective-permute-start.3
  236.5 74.3 %copy-start.5 = (s32[16,2]{0,1:T(2,128)S(1)}, s32[16,2]{0,1:T(2,128)}, u32[]{:S(2)}) copy-start(s32[16,2]{0,1:T(2,128)} %param.9) | copy-start | bytes 388
Sparse Core Ops, SparseCore 0:
  15.0 145.1 all-reduce.2
  210.1 100.7 all-gather.1
where the time goes:
time: 2070 us; the launch traced here: 2030 us
  local copies, waits for them, and re-layouts  1410 us (68%)
  loops' own time  332 us (16%)
  waiting for transfers between devices  221 us (11%)
  starting transfers between devices  28.4 us (1%)
  other arithmetic  24.7 us (1%)
    dynamic_update_slice x256, local copies, waits for them, and re-layouts, put_one(): lax.dynamic_update_slice(canvas_inner, piece, (zero_start, top_at, left_at))  985 us
    another operation x1, loops' own time, shards(): filled = lax.fori_loop(0, item_count, put_one, canvas)  332 us
    squeeze x256, local copies, waits for them, and re-layouts, put_one(): piece = lax.dynamic_index_in_dim(pieces, item, 0, keepdims=False)  232 us
    slice x256, local copies, waits for them, and re-layouts, put_one(): anchor[0, 1] - col_base + foot_cols  148 us
    psum x1, waiting for transfers between devices, shards(): cycle_every = lax.psum(contrib, ('grp', 'dev'))  138 us
    all_gather x1, waiting for transfers between devices, shards(): pieces = lax.all_gather(averages, ('grp', 'dev'), axis=0, tiled=True)  72.8 us
  transfers between devices with their start and end apart: 12, of which 7 were waited for; matrix products, arithmetic and copies ran while one was open for 1% of the time, Pallas kernels for 0%

commit v1 on v0

--- a/solution.py
+++ b/solution.py
@@ -99,7 +99,8 @@
     south_part = jnp.einsum("nkx,cnx->cnk", col_span, row_values[:, :nest_count], precision=highest)
     north_part = jnp.einsum("nkx,cnx->cnk", col_span, row_values[:, nest_count:], precision=highest)
     contrib = jnp.concatenate([west_part, east_part, south_part, north_part], axis=2)
-    cycle_every = lax.psum(contrib, ("grp", "dev"))
+    parts = lax.all_gather(contrib, ("grp", "dev"), axis=0, tiled=False)
+    cycle_every = parts.sum(axis=0)
     cycle_local = lax.dynamic_slice_in_dim(cycle_every, grp_index * local_nests, local_nests, 1)
     cycle_local = jnp.swapaxes(cycle_local, 0, 1)
     west_fine = jnp.repeat(cycle_local[:, :, :foot_rows], 3, axis=2)

time: 2070 us -> 2170 us (1.048)
  waiting for transfers between devices: 221 us -> 296 us
  other arithmetic: 24.7 us -> 55.6 us
    all_gather x0 -> x1, waiting for transfers between devices: none -> 216 us  [shards(): parts = lax.all_gather(contrib, ('grp', 'dev'), axis=0, tiled=False)]
    psum x1 -> x0, waiting for transfers between devices: 138 us -> none  [shards(): cycle_every = lax.psum(contrib, ('grp', 'dev'))]
    reduce_sum x0 -> x1, other arithmetic: none -> 30.6 us  [shards(): cycle_every = parts.sum(axis=0)]
  transfers between devices with their start and end apart: 12 -> 12, of which waited for: 7 -> 7; matrix products, arithmetic and copies ran while one was open for 1% -> 2% of each run, Pallas kernels for 0% -> 0%
where the time goes in v1:
time: 2170 us; the launch traced here: 2130 us
  local copies, waits for them, and re-layouts  1400 us (65%)
  loops' own time  334 us (15%)
  waiting for transfers between devices  296 us (14%)
  other arithmetic  55.6 us (3%)
  starting transfers between devices  28.2 us (1%)
    dynamic_update_slice x256, local copies, waits for them, and re-layouts, put_one(): lax.dynamic_update_slice(canvas_inner, piece, (zero_start, top_at, left_at))  985 us
    another operation x1, loops' own time, shards(): filled = lax.fori_loop(0, item_count, put_one, canvas)  334 us
    squeeze x256, local copies, waits for them, and re-layouts, put_one(): piece = lax.dynamic_index_in_dim(pieces, item, 0, keepdims=False)  232 us
    all_gather x1, waiting for transfers between devices, shards(): parts = lax.all_gather(contrib, ('grp', 'dev'), axis=0, tiled=False)  216 us
    slice x256, local copies, waits for them, and re-layouts, put_one(): anchor[0, 1] - col_base + foot_cols  138 us
    all_gather x1, waiting for transfers between devices, shards(): pieces = lax.all_gather(averages, ('grp', 'dev'), axis=0, tiled=True)  71 us
  transfers between devices with their start and end apart: 12, of which 7 were waited for; matrix products, arithmetic and copies ran while one was open for 2% of the time, Pallas kernels for 0%

profile of v1, /device:TPU:95, one launch (start us, length us, event | category | flops | bytes accessed | tf_op | source)
XLA Modules:
  0.0 2134.6 jit_solution(7152141047967232105)
XLA Ops:
  22.0 216.2 %all-gather.6.cloned.1.call-done = f32[3072,16,512]{2,0,1:T(8,128)} async-done(((f32[24,16,512]{2,0,1:T(8,128)}), f32[3072,16,512]{2,0,1:T(8,128)}) %all-gather.6.cloned.1.call-update) | async-done | bytes 100663312 | tf_op jit(solution)/shard_map/all_gather | solution.py:102
  238.2 30.6 %reduce_sum.18 = f32[24,16,512]{2,0,1:T(8,128)S(1)} reduce(f32[128,24,16,512]{3,1,0,2:T(8,128)} %bitcast.23, f32[]{:T(128)} %constant.219.clone.1), dimensions={0}, to_apply=%region_0.0 | reduce | flops 24969216 | bytes 101449728 | tf_op jit(solution)/shard_map/reduce_sum | solution.py:103
  296.8 8.9 copy.158
  305.7 10.2 reduce_sum.19
  347.9 71.0 %all-gather.4.cloned.1.call-done = f32[256,24,8,128]{3,2,1,0:T(8,128)} async-done(((f32[2,24,8,128]{3,2,1,0:T(8,128)}), f32[256,24,8,128]{3,2,1,0:T(8,128)}) %all-gather.4.cloned.1.call-update) | async-done | bytes 25165840 | tf_op jit(solution)/shard_map/all_gather | solution.py:136
  418.9 1706.7 %while.16 = (s32[]{:T(128)}, f32[24,80,384]{2,1,0:T(8,128)}, f32[256,24,8,128]{3,2,1,0:T(8,128)}, s32[16,2]{0,1:T(2,128)S(1)}, s32[]{:T(128)}, /*index=5*/s32[]{...) while((s32[]{:T(128)}, f32[24,80,384]{2,1,0:T(8,128)}, ...), condition=%wide.region_3.4_spmd, body=%wide.region_2.3_spmd.sunk | while | flops 46 | bytes 393888 | solution.py:151
  612.8 8.7 dynamic_update_slice.12
  630.3 8.7 dynamic_update_slice.12
  647.8 8.7 dynamic_update_slice.12
  665.3 8.7 dynamic_update_slice.12
  682.8 8.7 dynamic_update_slice.12
  700.3 8.7 dynamic_update_slice.12
  717.8 8.7 dynamic_update_slice.12
  735.3 8.7 dynamic_update_slice.12
  752.8 8.7 dynamic_update_slice.12
  770.3 8.7 dynamic_update_slice.12
  787.7 8.7 dynamic_update_slice.12
  805.2 8.7 dynamic_update_slice.12
  822.7 8.7 dynamic_update_slice.12
  1089.7 8.7 dynamic_update_slice.12
  1124.7 8.7 dynamic_update_slice.12
  1142.1 8.7 dynamic_update_slice.12
  1177.1 8.7 dynamic_update_slice.12
  1194.6 8.7 dynamic_update_slice.12
  1212.1 8.7 dynamic_update_slice.12
  1229.6 8.7 dynamic_update_slice.12
  1247.1 8.7 dynamic_update_slice.12
  1264.6 8.7 dynamic_update_slice.12
  1299.6 8.7 dynamic_update_slice.12
  1317.1 8.7 dynamic_update_slice.12
  1334.6 8.7 dynamic_update_slice.12
  1352.1 8.7 dynamic_update_slice.12
  (1105 shorter events, 1223.2 us)
Async XLA Ops:
  7.2 4.3 copy-start
  7.2 231.0 %all-gather.6.cloned.1.call-start = ((), (), s32[]{:S(2)}) async-start(), calls=%async_computation.1 | async-start | bytes 101449728 | tf_op jit(solution)/shard_map/all_gather | solution.py:102
  11.9 3.1 copy-start.4
  14.9 7.1 copy-start.7
  14.9 7.1 copy-start.6
  14.9 404.0 %all-gather.4.cloned.1.call-start = ((), (), s32[]{:S(2)}) async-start(), calls=%async_computation | async-start | bytes 25362432 | tf_op jit(solution)/shard_map/all_gather | solution.py:136
  15.3 1.2 copy-start.3
  16.5 255.2 %collective-permute-start.4 = (f32[2,24,1,384]{3,1,2,0:T(8,128)S(1)}, f32[2,24,1,384]{3,1,2,0:T(8,128)S(1)}, u32[]{:S(2)}, u32[]{:S(2)}) collective-permute-start(f32[2,24,1,384]{3,1,2,0:T(8,128)S(1)} %get-tuple-element.229), channel_id=1, source_target_pairs={{0,1},{1,2},{2,3},{3,4},{4,5},{5,6},{6,7},{7,8},{8,9},{9,10},{10,1... | collective-permute-start | bytes 221192 | tf_op jit(solution)/shard_map/ppermute | solution.py:14
  19.8 252.0 %collective-permute-start.5 = (f32[2,24,1,384]{3,1,2,0:T(8,128)S(1)}, f32[2,24,1,384]{3,1,2,0:T(8,128)S(1)}, u32[]{:S(2)}, u32[]{:S(2)}) collective-permute-start(f32[2,24,1,384]{3,1,2,0:T(8,128)S(1)} %get-tuple-element.230), channel_id=1, source_target_pairs={{1,0},{2,1},{3,2},{4,3},{5,4},{6,5},{7,6},{8,7},{9,8},{10,9},{11,1... | collective-permute-start | bytes 221192 | tf_op jit(solution)/shard_map/ppermute | solution.py:15
  271.7 12.8 copy-start.1
  276.0 5.5 collective-permute-start.6
  279.1 5.1 collective-permute-start.7
  286.8 5.6 collective-permute-start.8
  288.7 5.9 copy-start.2
  288.7 5.5 collective-permute-start.9
  318.1 6.4 collective-permute-start
  319.4 5.9 collective-permute-start.1
  328.4 7.1 collective-permute-start.2
  333.5 7.0 collective-permute-start.3
  346.4 72.5 %copy-start.5 = (s32[16,2]{0,1:T(2,128)S(1)}, s32[16,2]{0,1:T(2,128)}, u32[]{:S(2)}) copy-start(s32[16,2]{0,1:T(2,128)} %param.9) | copy-start | bytes 388
Sparse Core Ops, SparseCore 0:
  15.0 223.1 all-gather.5
  318.2 100.6 all-gather.3

commit v2 on v0

--- a/solution.py
+++ b/solution.py
@@ -132,7 +132,10 @@
     per_group = local_nests * dev_count
     zero_start = jnp.zeros((), jnp.int32)
     canvas = jnp.pad(advanced, ((0, 0), (coarse_rows, coarse_rows), (foot_cols, foot_cols)))
-    pieces = lax.all_gather(averages, ("grp", "dev"), axis=0, tiled=True)
+    peers = lax.axis_size(("grp", "dev"))
+    shards_2 = jnp.stack([averages for _ in range(peers)])
+    shards_2 = lax.all_to_all(shards_2, ("grp", "dev"), split_axis=0, concat_axis=0)
+    pieces = jnp.concatenate(shards_2, axis=0)
     item_count = pieces.shape[0]
 
     def put_one(item, canvas_inner):

time: 2070 us -> 2340 us (1.13)
  the two profiles are of different devices: /device:TPU:95 before, /device:TPU:127 now
where the time goes in v2:
time: 2340 us; the launch traced here: 2310 us
  local copies, waits for them, and re-layouts  1410 us (60%)
  waiting for transfers between devices  493 us (21%)
  loops' own time  310 us (13%)
  starting transfers between devices  44.7 us (2%)
  other arithmetic  24 us (1%)
    dynamic_update_slice x256, local copies, waits for them, and re-layouts, put_one(): lax.dynamic_update_slice(canvas_inner, piece, (zero_start, top_at, left_at))  987 us
    another operation x1, loops' own time, shards(): filled = lax.fori_loop(0, item_count, put_one, canvas)  310 us
    squeeze x256, local copies, waits for them, and re-layouts, put_one(): piece = lax.dynamic_index_in_dim(pieces, item, 0, keepdims=False)  232 us
    all_to_all x1, waiting for transfers between devices, shards(): lax.all_to_all(shards_2, ('grp', 'dev'), split_axis=0, concat_axis=0)  209 us
    ppermute x5, waiting for transfers between devices, padded_2(): after = lax.ppermute(initial, axis, down)  146 us
    slice x256, local copies, waits for them, and re-layouts, put_one(): anchor[0, 1] - col_base + foot_cols  139 us
    psum x1, waiting for transfers between devices, shards(): cycle_every = lax.psum(contrib, ('grp', 'dev'))  138 us
  transfers between devices with their start and end apart: 12, of which 6 were waited for; matrix products, arithmetic and copies ran while one was open for 1% of the time, Pallas kernels for 0%

profile of v2, /device:TPU:127, one launch (start us, length us, event | category | flops | bytes accessed | tf_op | source)
XLA Modules:
  0.0 2305.8 jit_solution(6446013359117400977)
XLA Ops:
  22.0 137.7 %all-reduce.3.cloned.1.call-done = f32[24,16,512]{2,0,1:T(8,128)} async-done(((f32[24,16,512]{2,0,1:T(8,128)}), f32[24,16,512]{2,0,1:T(8,128)}) %all-reduce.3.cloned.1.call-update) | async-done | bytes 786448 | tf_op jit(solution)/shard_map/psum | solution.py:102
  186.7 8.8 copy.162
  195.4 10.2 reduce_sum.9
  207.2 11.5 stack.2
  218.7 20.1 all-to-all-start
  250.9 142.9 %collective-permute-done.2 = f32[24,66,1]{1,0,2:T(8,128)S(1)} collective-permute-done((f32[24,66,1]{1,0,2:T(8,128)S(1)}, f32[24,66,1]{1,0,2:T(8,128)S(1)}, u32[]{:S(2)}, u32[]{:S(2)}) %collective-permute-start.2) | collective-permute-done | bytes 6368 | tf_op jit(solution)/shard_map/ppermute | solution.py:15
  401.1 208.5 %all-to-all-done = f32[128,2,24,8,128]{4,3,2,1,0:T(8,128)} async-done(((f32[128,2,24,8,128]{4,3,2,1,0:T(8,128)}), f32[128,2,24,8,128]{4,3,2,1,0:T(8,128)}, u32[]{:S(2)}, u32[]{:S(2)}) %all-to-all-start) | async-done | bytes 25165856 | tf_op jit(solution)/shard_map/all_to_all | solution.py:137
  609.7 1687.2 %while.16 = (s32[]{:T(128)}, f32[24,80,384]{2,1,0:T(8,128)}, f32[256,24,8,128]{3,2,1,0:T(8,128)}, s32[16,2]{0,1:T(2,128)S(1)}, s32[]{:T(128)}, /*index=5*/s32[]{...) while((s32[]{:T(128)}, f32[24,80,384]{2,1,0:T(8,128)}, ...), condition=%wide.region_3.4_spmd, body=%wide.region_2.3_spmd.sunk | while | flops 46 | bytes 393888 | solution.py:153
  801.4 8.6 dynamic_update_slice.12
  818.7 8.6 dynamic_update_slice.12
  836.0 8.6 dynamic_update_slice.12
  853.3 8.6 dynamic_update_slice.12
  870.5 8.6 dynamic_update_slice.12
  887.8 8.6 dynamic_update_slice.12
  905.1 8.6 dynamic_update_slice.12
  939.7 8.6 dynamic_update_slice.12
  956.9 8.6 dynamic_update_slice.12
  974.2 8.6 dynamic_update_slice.12
  991.5 8.6 dynamic_update_slice.12
  1008.8 8.6 dynamic_update_slice.12
  1026.1 8.7 dynamic_update_slice.12
  1043.4 8.7 dynamic_update_slice.12
  1272.9 8.6 dynamic_update_slice.12
  1290.1 8.6 dynamic_update_slice.12
  1307.4 8.6 dynamic_update_slice.12
  1324.7 8.6 dynamic_update_slice.12
  1342.0 8.6 dynamic_update_slice.12
  1376.5 8.6 dynamic_update_slice.12
  1393.8 8.6 dynamic_update_slice.12
  1411.1 8.6 dynamic_update_slice.12
  1428.4 8.6 dynamic_update_slice.12
  1445.7 8.6 dynamic_update_slice.12
  (1104 shorter events, 1233.6 us)
Async XLA Ops:
  7.2 4.3 copy-start
  7.2 152.6 %all-reduce.3.cloned.1.call-start = ((), (), s32[]{:S(2)}) async-start(), calls=%async_computation.1 | async-start | bytes 1572864 | tf_op jit(solution)/shard_map/psum | solution.py:102
  11.9 3.0 copy-start.4
  14.9 7.0 copy-start.7
  14.9 7.1 copy-start.6
  15.3 1.2 copy-start.3
  16.5 147.0 %collective-permute-start.4 = (f32[2,24,1,384]{3,1,2,0:T(8,128)S(1)}, f32[2,24,1,384]{3,1,2,0:T(8,128)S(1)}, u32[]{:S(2)}, u32[]{:S(2)}) collective-permute-start(f32[2,24,1,384]{3,1,2,0:T(8,128)S(1)} %get-tuple-element.229), channel_id=1, source_target_pairs={{0,1},{1,2},{2,3},{3,4},{4,5},{5,6},{6,7},{7,8},{8,9},{9,10},{10,1... | collective-permute-start | bytes 221192 | tf_op jit(solution)/shard_map/ppermute | solution.py:14
  17.8 145.7 %collective-permute-start.5 = (f32[2,24,1,384]{3,1,2,0:T(8,128)S(1)}, f32[2,24,1,384]{3,1,2,0:T(8,128)S(1)}, u32[]{:S(2)}, u32[]{:S(2)}) collective-permute-start(f32[2,24,1,384]{3,1,2,0:T(8,128)S(1)} %get-tuple-element.230), channel_id=1, source_target_pairs={{1,0},{2,1},{3,2},{4,3},{5,4},{6,5},{7,6},{8,7},{9,8},{10,9},{11,1... | collective-permute-start | bytes 221192 | tf_op jit(solution)/shard_map/ppermute | solution.py:15
  163.5 11.3 copy-start.1
  167.7 5.3 collective-permute-start.6
  169.0 5.4 collective-permute-start.7
  177.0 6.0 collective-permute-start.8
  178.3 6.2 copy-start.2
  178.3 5.9 collective-permute-start.9
  218.7 391.0 %all-to-all-start = ((f32[128,2,24,8,128]{4,3,2,1,0:T(8,128)}), f32[128,2,24,8,128]{4,3,2,1,0:T(8,128)}, u32[]{:S(2)}, u32[]{:S(2)}) async-start(f32[128,2,24,8,128]{4,3,2,1,0:T(8,128)} %stack.2), calls=%async_computation | async-start | bytes 50331648 | tf_op jit(solution)/shard_map/all_to_all | solution.py:137
  238.8 4.3 collective-permute-start
  240.1 3.9 collective-permute-start.1
  246.8 147.0 %collective-permute-start.2 = (f32[24,66,1]{1,0,2:T(8,128)S(1)}, f32[24,66,1]{1,0,2:T(8,128)S(1)}, u32[]{:S(2)}, u32[]{:S(2)}) collective-permute-start(f32[24,66,1]{1,0,2:T(8,128)S(1)} %copy.133), channel_id=1, source_target_pairs={{1,0},{2,1},{3,2},{4,3},{5,4},{6,5},{7,6},{8,7},{9,8},{10,9},{11,1... | collective-permute-start | bytes 19016 | tf_op jit(solution)/shard_map/ppermute | solution.py:15
  249.3 144.8 %collective-permute-start.3 = (f32[24,66,1]{1,0,2:T(8,128)S(1)}, f32[24,66,1]{1,0,2:T(8,128)S(1)}, u32[]{:S(2)}, u32[]{:S(2)}) collective-permute-start(f32[24,66,1]{1,0,2:T(8,128)S(1)} %copy.135), channel_id=1, source_target_pairs={{0,1},{1,2},{2,3},{3,4},{4,5},{5,6},{6,7},{7,8},{8,9},{9,10},{10,1... | collective-permute-start | bytes 19016 | tf_op jit(solution)/shard_map/ppermute | solution.py:14
  399.6 210.1 %copy-start.5 = (s32[16,2]{0,1:T(2,128)S(1)}, s32[16,2]{0,1:T(2,128)}, u32[]{:S(2)}) copy-start(s32[16,2]{0,1:T(2,128)} %param.9) | copy-start | bytes 388
Sparse Core Ops, SparseCore 0:
  15.0 144.6 all-reduce.2
